TPU v7x, 32 devices: a whole 2x2x4 slice. The times are simulated.
32 devices in a mesh: tile: 8 (over z, y), rec: 4 (over x, core).
Axes of the slice: x: 2, y: 2, z: 4, core: 2. Of those that a mesh axis runs over, the one named last changes fastest.
Arguments:
- screens: bfloat16 [2, 384, 128, 128], P(None, 'tile', 'rec'), may hold values from -1.796875 to 1.796875
- tile_owner: int32 [2, 2, 1024, 1], replicated, may hold values from 0 to 7; in each aligned block of 128 rows (0 to 127, 128 to 255, ..., all dimensions but the last counted through in order) at most 24 rows name the same one
- tile_slot: int32 [2, 2, 1024], replicated, may hold values from 0 to 47
- commands_init: float32 [4096], P('rec'), may hold values from -1.2 to 1.2
- reconstructor: bfloat16 [32, 16, 128, 128], P('rec', 'tile'), may hold values from -1 to 1
- pattern: int32 [32, 16], P('rec', 'tile'), may hold values from 0 to 31
Outputs:
- lgs_slopes: float32 [2, 32, 128], P(None, 'tile', 'rec')
- science_residual: bfloat16 [2, 992, 128, 128], P(None, 'tile', 'rec')
- commands: float32 [4096], P('rec')
Inputs may be any that keep to these rules, and one draw needn't show every extreme that they name: `tile_owner`: within the 128 consecutive entries of one index of tile for one frame and layer, each holder is named at most 24 times; in every frame and layer some such entries name one holder exactly 24 times.
All inputs are finite; a program needn't handle non-finite values.
Results may differ from a plain program's by a relative error of at most 0.011.
Values may be sent and summed in bfloat16 or wider, within the bound.
No kernel may reach another device: no remote copies, remote signals or barrier semaphores. Data moves between devices by JAX's collectives and lax.ppermute only.
A program may use at most 64 MiB of HBM per device.

v0:
```python
import math
import jax
import jax.numpy as jnp
from jax import lax
from jax.sharding import PartitionSpec as P

SUBPX = 16
SPOT = 32
SUB = 8
PT = 64
LG_DEV = 4
SC_DEV = 124
loop_gain = 0.5


def influence(tile_px, sub_px, sub_count):
    pixel = jnp.arange(tile_px, dtype=jnp.float32)[:, None] + 0.5
    centre = (jnp.arange(sub_count, dtype=jnp.float32)[None, :] + 0.5) * sub_px
    return jnp.maximum(0.0, 1.0 - jnp.abs(pixel - centre) / sub_px)


def tables(spot_px, sub_px):
    freq = jnp.arange(spot_px, dtype=jnp.int32)[:, None]
    pixel = jnp.arange(sub_px, dtype=jnp.int32)[None, :]
    turns = (freq * pixel % spot_px).astype(jnp.float32) * (2.0 * math.pi / spot_px)
    return (jnp.cos(turns).astype(jnp.bfloat16), jnp.sin(turns).astype(jnp.bfloat16))


def centred(spot_px):
    index = jnp.arange(spot_px, dtype=jnp.int32)
    return ((index + spot_px // 2) % spot_px - spot_px // 2).astype(jnp.float32) / spot_px


def along_pixels(values, table):
    return jnp.einsum("iaubv,nv->iaubn", values, table, preferred_element_type=jnp.float32)


def along_rows(table, values):
    return jnp.einsum("mu,iaubn->iabmn", table, values, preferred_element_type=jnp.float32)


def spot_slopes(residual):
    item_count, row_px, col_px = residual.shape
    sub_rows = row_px // SUBPX
    sub_cols = col_px // SUBPX
    cos_t, sin_t = tables(SPOT, SUBPX)
    pieces = residual.reshape(item_count, sub_rows, SUBPX, sub_cols, SUBPX)
    real_part = jnp.cos(pieces).astype(jnp.bfloat16)
    imag_part = jnp.sin(pieces).astype(jnp.bfloat16)
    g_re = (along_pixels(real_part, cos_t) + along_pixels(imag_part, sin_t)).astype(jnp.bfloat16)
    g_im = (along_pixels(imag_part, cos_t) - along_pixels(real_part, sin_t)).astype(jnp.bfloat16)
    h_re = along_rows(cos_t, g_re) + along_rows(sin_t, g_im)
    h_im = along_rows(cos_t, g_im) - along_rows(sin_t, g_re)
    spots = h_re * h_re + h_im * h_im
    coords = centred(SPOT)
    totals = jnp.sum(spots, axis=(3, 4))
    slope_x = jnp.sum(spots * coords[None, None, None, None, :], axis=(3, 4)) / totals
    slope_y = jnp.sum(spots * coords[None, None, None, :, None], axis=(3, 4)) / totals
    return jnp.stack([slope_x, slope_y], axis=-1).reshape(item_count, sub_rows * sub_cols * 2)


def pack_tiles(screens, owners, slots, pairs, my_tile, capacity):
    packed = []
    places = jnp.arange(capacity, dtype=jnp.int32)
    for frame, layer_idx in pairs:
        owner_rows = owners[frame, layer_idx]
        slot_rows = slots[frame, layer_idx]
        mine = owner_rows == my_tile
        order = jnp.cumsum(mine.astype(jnp.int32), axis=1) - 1
        picked = mine[:, None, :] & (order[:, None, :] == places[None, :, None])
        wanted = jnp.sum(jnp.where(picked, slot_rows[:, None, :], 0), axis=2)
        packed.append(jnp.take(screens[layer_idx], wanted, axis=0))
    return jnp.stack(packed, axis=1)


def unpack_tiles(received, owners, pairs, my_tile, capacity):
    results = []
    item_count = owners.shape[3]
    later = jnp.arange(item_count, dtype=jnp.int32)
    earlier_mask = later[None, :] < later[:, None]
    for position in range(len(pairs)):
        frame, layer_idx = pairs[position]
        mine = lax.dynamic_index_in_dim(owners[frame, layer_idx], my_tile, 0, keepdims=False)
        same_owner = mine[:, None] == mine[None, :]
        order = jnp.sum((same_owner & earlier_mask).astype(jnp.int32), axis=1)
        flat_index = mine * capacity + order
        layer_tiles = received[:, position].reshape(-1, received.shape[3], received.shape[4])
        results.append(jnp.take(layer_tiles, flat_index, axis=0).astype(jnp.float32))
    return results


def add_layers(pieces, first_index):
    phase = pieces[first_index]
    phase = phase + pieces[first_index + 1]
    return phase


def per_device(screens, tile_owner, tile_slot, commands_init, reconstructor, pattern):
    layer_total, tiles_here, slab_rows, tile_px = screens.shape
    frame_total = tile_owner.shape[0]
    tile_count = lax.axis_size("tile")
    rec_count = lax.axis_size("rec")
    my_tile = lax.axis_index("tile")
    my_rec = lax.axis_index("rec")
    item_count = LG_DEV + SC_DEV
    capacity = max(2, 3 * item_count // (2 * tile_count))
    owners = tile_owner[..., 0].reshape(frame_total, layer_total, tile_count, item_count)
    slots = tile_slot.reshape(frame_total, layer_total, tile_count, item_count)
    influence_all = influence(tile_px, SUBPX, SUB)
    influence_rows = lax.dynamic_slice_in_dim(influence_all, my_rec * slab_rows, slab_rows, 0)
    lgs_places = (my_tile * LG_DEV + jnp.arange(LG_DEV, dtype=jnp.int32)) % PT
    sci_places = (my_tile * SC_DEV + jnp.arange(SC_DEV, dtype=jnp.int32)) % PT
    item_places = jnp.concatenate([lgs_places, sci_places])
    state = commands_init
    slope_frames = []
    science_frames = []
    for frame in range(frame_total):
        pairs = [(frame, layer_idx) for layer_idx in range(layer_total)]
        sending = pack_tiles(screens, owners, slots, pairs, my_tile, capacity)
        received = lax.all_to_all(sending, "tile", split_axis=0, concat_axis=0, tiled=True)
        pieces = unpack_tiles(received, owners, pairs, my_tile, capacity)
        phase = add_layers(pieces, 0)
        full_commands = lax.all_gather(state, "rec", axis=0, tiled=True)
        mirror = full_commands.reshape(PT, SUB, SUB)
        chosen = jnp.take(mirror, item_places, axis=0)
        shapes = jnp.einsum(
            "xa,iab,yb->ixy", influence_rows, chosen, influence_all, precision=lax.Precision.HIGHEST
        )
        residual = phase - shapes
        science_frames.append(residual[LG_DEV:].astype(jnp.bfloat16))
        slopes = spot_slopes(residual[:LG_DEV])
        slope_frames.append(slopes)
        slopes_b = slopes.astype(jnp.bfloat16)
        everyone = lax.all_gather(slopes_b[None], ("tile", "rec"), axis=0, tiled=True)
        everyone = everyone.reshape(tile_count, rec_count, LG_DEV, -1).transpose(0, 2, 1, 3)
        everyone = everyone.reshape(tile_count * LG_DEV, -1)
        needed = jnp.take(everyone, pattern, axis=0)
        partial_rows = jnp.einsum(
            "ibcs,ibs->ic", reconstructor, needed, preferred_element_type=jnp.float32
        ).reshape(-1)
        state = state + loop_gain * lax.psum(partial_rows, "tile")
    return (jnp.stack(slope_frames, axis=0), jnp.stack(science_frames, axis=0), state)


def solution(mesh):
    placed = (
        P(None, "tile", "rec", None),
        P(),
        P(),
        P("rec"),
        P("rec", "tile", None, None),
        P("rec", "tile"),
    )
    return jax.shard_map(
        per_device,
        mesh=mesh,
        in_specs=placed,
        out_specs=(P(None, "tile", "rec"), P(None, "tile", "rec", None), P("rec")),
        check_vma=False,
    )
```

profile of v0, /device:TPU:0, one launch (start us, length us, event | category | flops | bytes accessed | tf_op | source)
XLA Modules:
  0.0 293.3 jit_solution(11876869289070020217)
XLA Ops:
  0.6 0.8 reshape.281
  1.5 0.7 fusion.160
  3.2 1.2 slice_bitcast_fusion.1
  4.5 0.9 gather_fusion.1
  5.4 1.4 select_bitcast_fusion.2
  6.9 0.9 gather_fusion
  8.1 1.1 copy-done.2
  9.2 2.0 pad_maximum_fusion
  11.2 7.3 %all-to-all-start = ((bf16[8,2,24,32,128]{4,3,2,1,0:T(8,128)(2,1)}), bf16[8,2,24,32,128]{4,3,2,1,0:T(8,128)(2,1)}, u32[]{:S(2)}, u32[]{:S(2)}) async-start(bf16[8,2,24,32,128]{4,3,2,1,0:T(8,128)(2,1)} %pad_maximum_fusion), calls=%async_computation | async-start | bytes 6291456 | tf_op jit(solution)/shard_map/all_to_all | solution.py:120
  19.5 0.9 gather_fusion.6
  20.5 2.0 gather_fusion.5
  22.5 5.2 %all_gather.12 = f32[4096]{0:T(1024)S(1)} all-gather(f32[1024]{0:T(1024)S(1)} %copy-done.6), channel_id=1, replica_groups=mesh['tile'=8,'rec'=4] {'rec'}, dimensions={0}, use_global_device_ids=true | all-gather | bytes 20480 | tf_op jit(solution)/shard_map/all_gather | solution.py:123
  27.9 0.8 gather_fusion.4
  29.9 1.1 copy-done.1
  31.3 2.0 pad_maximum_fusion.1
  33.5 55.7 %all-to-all-done = bf16[8,2,24,32,128]{4,3,2,1,0:T(8,128)(2,1)} async-done(((bf16[8,2,24,32,128]{4,3,2,1,0:T(8,128)(2,1)}), bf16[8,2,24,32,128]{4,3,2,1,0:T(8,128)(2,1)}, u32[]{:S(2)}, u32[]{:S(2)}) %all-to-all-start) | async-done | bytes 3145760 | tf_op jit(solution)/shard_map/all_to_all | solution.py:120
  89.3 4.7 %all-to-all-start.1 = ((bf16[8,2,24,32,128]{4,3,2,1,0:T(8,128)(2,1)}), bf16[8,2,24,32,128]{4,3,2,1,0:T(8,128)(2,1)}, u32[]{:S(2)}, u32[]{:S(2)}) async-start(bf16[8,2,24,32,128]{4,3,2,1,0:T(8,128)(2,1)} %pad_maximum_fusion.1), calls=%async_computation.1 | async-start | bytes 6291456 | tf_op jit(solution)/shard_map/all_to_all | solution.py:120
  94.5 0.4 fusion.54
  94.9 3.7 %fusion.164 = (bf16[8,1,24,32,128]{4,3,2,1,0:T(8,128)(2,1)S(1)}, bf16[8,1,24,32,128]{4,3,2,1,0:T(8,128)(2,1)}) fusion(bf16[8,2,24,32,128]{4,3,2,1,0:T(8,128)(2,1)} %all-to-all-done), kind=kLoop, calls=%fused_computation.284 | loop fusion | bytes 6291456 | tf_op jit(solution)/shard_map/slice | solution.py:87
  98.6 2.2 gather_fusion.3
  100.8 1.7 gather_fusion.2
  102.5 5.7 %add_subtract_fusion.1 = f32[128,32,128]{2,0,1:T(8,128)S(1)} fusion(bf16[128,32,128]{2,1,0:T(8,128)(2,1)S(1)} %gather_fusion.3, bf16[128,32,128]{2,1,0:T(8,128)(2,1)} %gather_fusion.2, pred[128]{0:T(512)(128)(4,1)S(1)} %get-tuple-element.29, pred[128]{0:T(512)(128)(4,1)S(1)} %get-tuple-element.73, f32[128,8,32]{0,2,1:T(8,128)S(1)} %fusion.54, ...), kind=kOutput, calls=%fused_computation.18 | convolution fusion | flops 53482496 | bytes 4326176 | tf_op jit(solution)/shard_map/xa,iab,yb->ixy/dot_general | solution.py:126
  108.1 0.5 cosine_convert_fusion.1
  108.6 0.9 copy-done.3
  111.8 0.4 fusion.2
  112.1 1.0 multiply_reduce_fusion.3
  113.4 65.8 %all_gather.13 = bf16[32,4,32]{2,1,0:T(4,128)(2,1)S(1)} all-gather(bf16[1,4,32]{2,1,0:T(4,128)(2,1)S(1)} %copy.90), channel_id=1, replica_groups=mesh['tile'=8,'rec'=4] {'tile','rec'}, dimensions={0}, use_global_device_ids=true | all-gather | bytes 8448 | tf_op jit(solution)/shard_map/all_gather | solution.py:134
  179.4 0.6 gather_fusion.9
  180.3 26.0 %psum.14 = f32[1024]{0:T(1024)S(1)} all-reduce(f32[1024]{0:T(1024)S(1)} %bitcast.175), channel_id=1, replica_groups=mesh['tile'=8,'rec'=4] {'tile'}, use_global_device_ids=true, to_apply=%region_15.20 | all-reduce | flops 1024 | bytes 8192 | tf_op jit(solution)/shard_map/psum | solution.py:141
  206.3 5.4 %all_gather.14 = f32[4096]{0:T(1024)S(1)} all-gather(f32[1024]{0:T(1024)S(1)} %multiply_add_fusion.1), channel_id=1, replica_groups=mesh['tile'=8,'rec'=4] {'rec'}, dimensions={0}, use_global_device_ids=true | all-gather | bytes 20480 | tf_op jit(solution)/shard_map/all_gather | solution.py:123
  211.9 0.8 gather_fusion.10
  213.1 0.4 fusion.52
  213.5 3.7 %fusion.165 = (bf16[8,1,24,32,128]{4,3,2,1,0:T(8,128)(2,1)S(1)}, bf16[8,1,24,32,128]{4,3,2,1,0:T(8,128)(2,1)}) fusion(bf16[8,2,24,32,128]{4,3,2,1,0:T(8,128)(2,1)} %all-to-all-done.1), kind=kLoop, calls=%fused_computation.285 | loop fusion | bytes 6291456 | tf_op jit(solution)/shard_map/slice | solution.py:87
  217.2 2.2 gather_fusion.8
  219.4 1.7 gather_fusion.7
  221.0 5.7 %add_subtract_fusion = f32[128,32,128]{2,0,1:T(8,128)S(1)} fusion(bf16[128,32,128]{2,1,0:T(8,128)(2,1)S(1)} %gather_fusion.8, bf16[128,32,128]{2,1,0:T(8,128)(2,1)} %gather_fusion.7, pred[128]{0:T(512)(128)(4,1)S(1)} %get-tuple-element.37, pred[128]{0:T(512)(128)(4,1)S(1)} %get-tuple-element.71, f32[128,8,32]{0,2,1:T(8,128)S(1)} %fusion.52, ...), kind=kOutput, calls=%fused_computation.17 | convolution fusion | flops 53482496 | bytes 4326176 | tf_op jit(solution)/shard_map/xa,iab,yb->ixy/dot_general | solution.py:126
  226.7 0.5 cosine_convert_fusion
  227.5 0.8 copy-done.4
  228.8 1.1 fusion.14
  230.3 1.3 fusion.11
  232.3 0.4 fusion.67
  233.1 0.9 multiply_reduce_fusion.1
  234.4 2.6 copy.106
  237.1 36.8 %all_gather.15 = bf16[32,4,32]{2,1,0:T(4,128)(2,1)S(1)} all-gather(bf16[1,4,32]{2,1,0:T(4,128)(2,1)S(1)} %copy.103), channel_id=1, replica_groups=mesh['tile'=8,'rec'=4] {'tile','rec'}, dimensions={0}, use_global_device_ids=true | all-gather | bytes 8448 | tf_op jit(solution)/shard_map/all_gather | solution.py:134
  274.1 0.6 gather_fusion.11
  275.0 17.1 %psum.15 = f32[1024]{0:T(1024)S(1)} all-reduce(f32[1024]{0:T(1024)S(1)} %bitcast.176), channel_id=1, replica_groups=mesh['tile'=8,'rec'=4] {'tile'}, use_global_device_ids=true, to_apply=%region_19.24 | all-reduce | flops 1024 | bytes 8192 | tf_op jit(solution)/shard_map/psum | solution.py:141
  292.1 0.6 multiply_add_fusion
  292.7 0.6 pad_maximum_fusion.5
  (116 shorter events, 11.5 us)
Async XLA Ops:
  0.6 179.4 %copy-start = (bf16[8,2,128,128]{3,2,1,0:T(8,128)(2,1)S(1)}, bf16[8,2,128,128]{3,2,1,0:T(8,128)(2,1)}, u32[]{:S(2)}) copy-start(bf16[8,2,128,128]{3,2,1,0:T(8,128)(2,1)} %param.18) | copy-start | bytes 1572868
  7.8 1.4 copy-start.2
  11.2 78.1 %all-to-all-start = ((bf16[8,2,24,32,128]{4,3,2,1,0:T(8,128)(2,1)}), bf16[8,2,24,32,128]{4,3,2,1,0:T(8,128)(2,1)}, u32[]{:S(2)}, u32[]{:S(2)}) async-start(bf16[8,2,24,32,128]{4,3,2,1,0:T(8,128)(2,1)} %pad_maximum_fusion), calls=%async_computation | async-start | bytes 6291456 | tf_op jit(solution)/shard_map/all_to_all | solution.py:120
  20.5 2.0 copy-start.6
  20.5 8.3 %copy-start.5 = (s32[2,2,1024,1]{2,3,1,0:T(1,128)S(1)}, s32[2,2,1024,1]{2,3,1,0:T(1,128)}, u32[]{:S(2)}) copy-start(s32[2,2,1024,1]{2,3,1,0:T(1,128)} %param.15) | copy-start | bytes 49156
  29.6 1.4 copy-start.1
  31.3 2.0 copy-start.7
  89.3 124.2 %all-to-all-start.1 = ((bf16[8,2,24,32,128]{4,3,2,1,0:T(8,128)(2,1)}), bf16[8,2,24,32,128]{4,3,2,1,0:T(8,128)(2,1)}, u32[]{:S(2)}, u32[]{:S(2)}) async-start(bf16[8,2,24,32,128]{4,3,2,1,0:T(8,128)(2,1)} %pad_maximum_fusion.1), calls=%async_computation.1 | async-start | bytes 6291456 | tf_op jit(solution)/shard_map/all_to_all | solution.py:120
  108.1 1.4 copy-start.3
  226.7 1.6 copy-start.4
where the time goes:
time: 294 us; the launch traced here: 293 us
  blocking collectives  156 us (53%)
  waiting for transfers between devices  55.7 us (19%)
  local copies, waits for them, and re-layouts  34.4 us (12%)
  matrix products  20.7 us (7%)
  other arithmetic  12.8 us (4%)
  starting transfers between devices  11.9 us (4%)
    all_gather x2, blocking collectives, per_device(): lax.all_gather(slopes_b[None], ('tile', 'rec'), axis=0, tiled=True)  103 us
    all_to_all x2, waiting for transfers between devices, per_device(): lax.all_to_all(sending, 'tile', split_axis=0, concat_axis=0, tiled=True)  55.7 us
    psum x2, blocking collectives, per_device(): state = state + loop_gain * lax.psum(partial_rows, 'tile')  43.2 us
    dot_general x4, matrix products, per_device(): jnp.einsum('xa,iab,yb->ixy', influence_rows, chosen, influence_all, preci...  12.2 us
    all_to_all x2, starting transfers between devices, per_device(): lax.all_to_all(sending, 'tile', split_axis=0, concat_axis=0, tiled=True)  11.9 us
    all_gather x2, blocking collectives, per_device(): full_commands = lax.all_gather(state, 'rec', axis=0, tiled=True)  10.6 us
    gather x4, local copies, waits for them, and re-layouts, unpack_tiles(): jnp.take(layer_tiles, flat_index, axis=0).astype(jnp.float32)  7.65 us
    slice x2, local copies, waits for them, and re-layouts, unpack_tiles(): received[:, position].reshape(-1, received.shape[3], received.shape[4])  7.41 us
  transfers between devices with their start and end apart: 2, of which 1 were waited for; matrix products, arithmetic and copies ran while one was open for 10% of the time, Pallas kernels for 0%

commit v1 on v0

--- a/solution.py
+++ b/solution.py
@@ -11,6 +11,11 @@
 LG_DEV = 4
 SC_DEV = 124
 loop_gain = 0.5
+
+
+def direct_map(s0, axis_id):
+    long_array = jnp.sum(lax.all_gather(s0, axis_name=axis_id), 0)
+    return long_array
 
 
 def influence(tile_px, sub_px, sub_count):
@@ -138,7 +143,7 @@
         partial_rows = jnp.einsum(
             "ibcs,ibs->ic", reconstructor, needed, preferred_element_type=jnp.float32
         ).reshape(-1)
-        state = state + loop_gain * lax.psum(partial_rows, "tile")
+        state = state + loop_gain * direct_map(partial_rows, axis_id="tile")
     return (jnp.stack(slope_frames, axis=0), jnp.stack(science_frames, axis=0), state)
 
 

time: 294 us -> 320 us (1.088)
  blocking collectives: 156 us -> 182 us
    all_gather x0 -> x2, blocking collectives: none -> 67.4 us  [direct_map(): long_array = jnp.sum(lax.all_gather(s0, axis_name=axis_id), 0)]
    psum x2 -> x0, blocking collectives: 43.2 us -> none  [per_device(): state = state + loop_gain * lax.psum(partial_rows, 'tile')]
  transfers between devices with their start and end apart: 2 -> 2, of which waited for: 1 -> 1; matrix products, arithmetic and copies ran while one was open for 10% -> 9% of each run, Pallas kernels for 0% -> 0%
where the time goes in v1:
time: 320 us; the launch traced here: 319 us
  blocking collectives  182 us (57%)
  waiting for transfers between devices  55.9 us (17%)
  local copies, waits for them, and re-layouts  34.4 us (11%)
  matrix products  20.7 us (6%)
  other arithmetic  12.8 us (4%)
  starting transfers between devices  11.9 us (4%)
    all_gather x2, blocking collectives, per_device(): lax.all_gather(slopes_b[None], ('tile', 'rec'), axis=0, tiled=True)  104 us
    all_gather x2, blocking collectives, direct_map(): long_array = jnp.sum(lax.all_gather(s0, axis_name=axis_id), 0)  67.4 us
    all_to_all x2, waiting for transfers between devices, per_device(): lax.all_to_all(sending, 'tile', split_axis=0, concat_axis=0, tiled=True)  55.9 us
    dot_general x4, matrix products, per_device(): jnp.einsum('xa,iab,yb->ixy', influence_rows, chosen, influence_all, preci...  12.2 us
    all_to_all x2, starting transfers between devices, per_device(): lax.all_to_all(sending, 'tile', split_axis=0, concat_axis=0, tiled=True)  11.9 us
    all_gather x2, blocking collectives, per_device(): full_commands = lax.all_gather(state, 'rec', axis=0, tiled=True)  10.6 us
    gather x4, local copies, waits for them, and re-layouts, unpack_tiles(): jnp.take(layer_tiles, flat_index, axis=0).astype(jnp.float32)  7.65 us
    slice x2, local copies, waits for them, and re-layouts, unpack_tiles(): received[:, position].reshape(-1, received.shape[3], received.shape[4])  7.41 us
  transfers between devices with their start and end apart: 2, of which 1 were waited for; matrix products, arithmetic and copies ran while one was open for 9% of the time, Pallas kernels for 0%

profile of v1, /device:TPU:0, one launch (start us, length us, event | category | flops | bytes accessed | tf_op | source)
XLA Modules:
  0.0 319.4 jit_solution(1998445765890395899)
XLA Ops:
  0.6 0.8 reshape.275
  1.5 0.7 fusion.158
  3.2 1.2 slice_bitcast_fusion.1
  4.5 0.9 gather_fusion.1
  5.4 1.4 select_bitcast_fusion.2
  6.9 0.9 gather_fusion
  8.1 1.1 copy-done.2
  9.2 2.0 pad_maximum_fusion
  11.2 7.3 %all-to-all-start = ((bf16[8,2,24,32,128]{4,3,2,1,0:T(8,128)(2,1)}), bf16[8,2,24,32,128]{4,3,2,1,0:T(8,128)(2,1)}, u32[]{:S(2)}, u32[]{:S(2)}) async-start(bf16[8,2,24,32,128]{4,3,2,1,0:T(8,128)(2,1)} %pad_maximum_fusion), calls=%async_computation | async-start | bytes 6291456 | tf_op jit(solution)/shard_map/all_to_all | solution.py:125
  19.5 0.9 gather_fusion.6
  20.5 2.0 gather_fusion.5
  22.5 5.2 %all_gather.18 = f32[4096]{0:T(1024)S(1)} all-gather(f32[1024]{0:T(1024)S(1)} %copy-done.6), channel_id=1, replica_groups=mesh['tile'=8,'rec'=4] {'rec'}, dimensions={0}, use_global_device_ids=true | all-gather | bytes 20480 | tf_op jit(solution)/shard_map/all_gather | solution.py:128
  27.9 0.8 gather_fusion.4
  29.7 1.1 copy-done.1
  31.1 2.0 pad_maximum_fusion.1
  33.3 55.9 %all-to-all-done = bf16[8,2,24,32,128]{4,3,2,1,0:T(8,128)(2,1)} async-done(((bf16[8,2,24,32,128]{4,3,2,1,0:T(8,128)(2,1)}), bf16[8,2,24,32,128]{4,3,2,1,0:T(8,128)(2,1)}, u32[]{:S(2)}, u32[]{:S(2)}) %all-to-all-start) | async-done | bytes 3145760 | tf_op jit(solution)/shard_map/all_to_all | solution.py:125
  89.3 4.7 %all-to-all-start.1 = ((bf16[8,2,24,32,128]{4,3,2,1,0:T(8,128)(2,1)}), bf16[8,2,24,32,128]{4,3,2,1,0:T(8,128)(2,1)}, u32[]{:S(2)}, u32[]{:S(2)}) async-start(bf16[8,2,24,32,128]{4,3,2,1,0:T(8,128)(2,1)} %pad_maximum_fusion.1), calls=%async_computation.1 | async-start | bytes 6291456 | tf_op jit(solution)/shard_map/all_to_all | solution.py:125
  95.1 3.7 %fusion.162 = (bf16[8,1,24,32,128]{4,3,2,1,0:T(8,128)(2,1)S(1)}, bf16[8,1,24,32,128]{4,3,2,1,0:T(8,128)(2,1)}) fusion(bf16[8,2,24,32,128]{4,3,2,1,0:T(8,128)(2,1)} %all-to-all-done), kind=kLoop, calls=%fused_computation.284 | loop fusion | bytes 6291456 | tf_op jit(solution)/shard_map/slice | solution.py:92
  98.8 2.2 gather_fusion.3
  101.0 1.7 gather_fusion.2
  102.6 5.7 %add_subtract_fusion.1 = f32[128,32,128]{2,0,1:T(8,128)S(1)} fusion(bf16[128,32,128]{2,1,0:T(8,128)(2,1)S(1)} %gather_fusion.3, bf16[128,32,128]{2,1,0:T(8,128)(2,1)} %gather_fusion.2, pred[128]{0:T(512)(128)(4,1)S(1)} %get-tuple-element.29, pred[128]{0:T(512)(128)(4,1)S(1)} %get-tuple-element.73, f32[128,8,32]{0,2,1:T(8,128)S(1)} %fusion.52, ...), kind=kOutput, calls=%fused_computation.18 | convolution fusion | flops 53482496 | bytes 4326176 | tf_op jit(solution)/shard_map/xa,iab,yb->ixy/dot_general | solution.py:131
  108.3 0.5 cosine_convert_fusion.1
  108.8 0.9 copy-done.3
  111.6 0.4 fusion.71
  111.9 0.4 fusion.2
  112.3 0.9 multiply_reduce_fusion.3
  113.6 65.7 %all_gather.19 = bf16[32,4,32]{2,1,0:T(4,128)(2,1)S(1)} all-gather(bf16[1,4,32]{2,1,0:T(4,128)(2,1)S(1)} %copy.90), channel_id=1, replica_groups=mesh['tile'=8,'rec'=4] {'tile','rec'}, dimensions={0}, use_global_device_ids=true | all-gather | bytes 8448 | tf_op jit(solution)/shard_map/all_gather | solution.py:139
  179.4 0.6 gather_fusion.9
  180.3 36.9 %all-gather = f32[8,1,1024]{2,1,0:T(1,128)S(1)} all-gather(f32[1,1,1024]{2,1,0:T(1,128)S(1)} %convolution_bitcast_fusion.1), channel_id=1, replica_groups=mesh['tile'=8,'rec'=4] {'tile'}, dimensions={0}, use_global_device_ids=true | all-gather | bytes 36864 | tf_op jit(solution)/shard_map/all_gather | solution.py:17
  217.3 5.4 %all_gather.21 = f32[4096]{0:T(1024)S(1)} all-gather(f32[1024]{0:T(1024)S(1)} %multiply_add_fusion.1), channel_id=1, replica_groups=mesh['tile'=8,'rec'=4] {'rec'}, dimensions={0}, use_global_device_ids=true | all-gather | bytes 20480 | tf_op jit(solution)/shard_map/all_gather | solution.py:128
  222.8 0.8 gather_fusion.10
  224.0 0.4 fusion.50
  224.4 3.7 %fusion.163 = (bf16[8,1,24,32,128]{4,3,2,1,0:T(8,128)(2,1)S(1)}, bf16[8,1,24,32,128]{4,3,2,1,0:T(8,128)(2,1)}) fusion(bf16[8,2,24,32,128]{4,3,2,1,0:T(8,128)(2,1)} %all-to-all-done.1), kind=kLoop, calls=%fused_computation.285 | loop fusion | bytes 6291456 | tf_op jit(solution)/shard_map/slice | solution.py:92
  228.1 2.2 gather_fusion.8
  230.3 1.7 gather_fusion.7
  232.0 5.7 %add_subtract_fusion = f32[128,32,128]{2,0,1:T(8,128)S(1)} fusion(bf16[128,32,128]{2,1,0:T(8,128)(2,1)S(1)} %gather_fusion.8, bf16[128,32,128]{2,1,0:T(8,128)(2,1)} %gather_fusion.7, pred[128]{0:T(512)(128)(4,1)S(1)} %get-tuple-element.37, pred[128]{0:T(512)(128)(4,1)S(1)} %get-tuple-element.71, f32[128,8,32]{0,2,1:T(8,128)S(1)} %fusion.50, ...), kind=kOutput, calls=%fused_computation.17 | convolution fusion | flops 53482496 | bytes 4326176 | tf_op jit(solution)/shard_map/xa,iab,yb->ixy/dot_general | solution.py:131
  237.7 0.5 cosine_convert_fusion
  238.4 0.8 copy-done.4
  239.8 1.1 fusion.14
  241.3 1.3 fusion.11
  243.2 0.4 fusion.65
  244.0 0.9 multiply_reduce_fusion.1
  245.4 2.6 copy.106
  248.1 38.6 %all_gather.22 = bf16[32,4,32]{2,1,0:T(4,128)(2,1)S(1)} all-gather(bf16[1,4,32]{2,1,0:T(4,128)(2,1)S(1)} %copy.103), channel_id=1, replica_groups=mesh['tile'=8,'rec'=4] {'tile','rec'}, dimensions={0}, use_global_device_ids=true | all-gather | bytes 8448 | tf_op jit(solution)/shard_map/all_gather | solution.py:139
  286.8 0.6 gather_fusion.11
  287.7 30.4 %all-gather.1 = f32[8,1,1024]{2,1,0:T(1,128)S(1)} all-gather(f32[1,1,1024]{2,1,0:T(1,128)S(1)} %convolution_bitcast_fusion), channel_id=1, replica_groups=mesh['tile'=8,'rec'=4] {'tile'}, dimensions={0}, use_global_device_ids=true | all-gather | bytes 36864 | tf_op jit(solution)/shard_map/all_gather | solution.py:17
  318.2 0.6 multiply_add_fusion
  318.8 0.6 pad_maximum_fusion.5
  (118 shorter events, 11.6 us)
Async XLA Ops:
  0.6 179.4 %copy-start = (bf16[8,2,128,128]{3,2,1,0:T(8,128)(2,1)S(1)}, bf16[8,2,128,128]{3,2,1,0:T(8,128)(2,1)}, u32[]{:S(2)}) copy-start(bf16[8,2,128,128]{3,2,1,0:T(8,128)(2,1)} %param.18) | copy-start | bytes 1572868
  7.8 1.4 copy-start.2
  11.2 78.1 %all-to-all-start = ((bf16[8,2,24,32,128]{4,3,2,1,0:T(8,128)(2,1)}), bf16[8,2,24,32,128]{4,3,2,1,0:T(8,128)(2,1)}, u32[]{:S(2)}, u32[]{:S(2)}) async-start(bf16[8,2,24,32,128]{4,3,2,1,0:T(8,128)(2,1)} %pad_maximum_fusion), calls=%async_computation | async-start | bytes 6291456 | tf_op jit(solution)/shard_map/all_to_all | solution.py:125
  20.5 2.0 copy-start.6
  20.5 8.3 %copy-start.5 = (s32[2,2,1024,1]{2,3,1,0:T(1,128)S(1)}, s32[2,2,1024,1]{2,3,1,0:T(1,128)}, u32[]{:S(2)}) copy-start(s32[2,2,1024,1]{2,3,1,0:T(1,128)} %param.15) | copy-start | bytes 49156
  29.4 1.4 copy-start.1
  31.1 2.0 copy-start.7
  89.3 135.2 %all-to-all-start.1 = ((bf16[8,2,24,32,128]{4,3,2,1,0:T(8,128)(2,1)}), bf16[8,2,24,32,128]{4,3,2,1,0:T(8,128)(2,1)}, u32[]{:S(2)}, u32[]{:S(2)}) async-start(bf16[8,2,24,32,128]{4,3,2,1,0:T(8,128)(2,1)} %pad_maximum_fusion.1), calls=%async_computation.1 | async-start | bytes 6291456 | tf_op jit(solution)/shard_map/all_to_all | solution.py:125
  108.3 1.4 copy-start.3
  237.7 1.6 copy-start.4
